TPU v7x, 512 devices: a whole 4x8x8 slice. The times are simulated.
512 devices in a mesh: lat: 32 (over y, x_hi, core), lon: 16 (over z, x_lo).
Axes of the slice: x: 4 (x_hi: 2, x_lo: 2; x = x_hi * 2 + x_lo), y: 8, z: 8, core: 2. Of those that a mesh axis runs over, the one named last changes fastest.
Arguments:
- tracers: float32 [5, 1, 3072, 2048], P(None, None, 'lat', 'lon'), may hold values from 0.2 to 2
- offsets: int32 [3072, 2048], P('lat', 'lon'), may hold values from 0 to 255, as said below
- fraction: float32 [3072, 2048], P('lat', 'lon'), may hold values from 0 to 0.95
- courant_north: float32 [3072, 2048], P('lat', 'lon'), may hold values from 0 to 0.9
Outputs:
- advected: float32 [5, 1, 3072, 2048], P(None, None, 'lat', 'lon')
Inputs may be any that keep to these rules, and one draw needn't show every extreme that they name: Let k = min(r, 3071 - r) for row r. Rows with k < 24 have offsets from 128 to 255, the largest reached in row 0; rows with 24 <= k < 48 have offsets at most 64, reached in row 24; all other rows have offsets at most 8, reached in row 48. Offsets of adjacent faces g and g + 1 of a row differ by at most one.
All inputs are finite; a program needn't handle non-finite values.
Results may differ from a plain program's by a relative error of at most 0.0003.
Values sent between devices are 32-bit elements; how exact they have to be, the bound alone decides.
A program may use at most 64 MiB of HBM per device.

v0:
```python
import jax
import jax.numpy as jnp
from jax import lax
from jax.sharding import PartitionSpec as P

wide_weight = 7.0 / 12.0
narrow_weight = 1.0 / 12.0


def with_halo(block, sides, width, periodic):
    for axis, dim in sides:
        count = lax.axis_size(axis)
        forward = [(i, i + 1) for i in range(count - 1)]
        if periodic:
            forward.append((count - 1, 0))
        backward = [(target, source) for source, target in forward]
        low = lax.ppermute(
            lax.slice_in_dim(block, block.shape[dim] - width, None, axis=dim), axis, forward
        )
        high = lax.ppermute(lax.slice_in_dim(block, 0, width, axis=dim), axis, backward)
        block = jnp.concatenate([low, block, high], axis=dim)
    return block


def shifted(value, axis, steps):
    count = lax.axis_size(axis)
    pairs = [(source, (source + steps) % count) for source in range(count)]
    return lax.ppermute(value, axis, pairs)


def frac_flux(courant, right_edge, edge_jump, curvature):
    return courant * (
        right_edge - 0.5 * courant * (edge_jump - (1.0 - 2.0 / 3.0 * courant) * curvature)
    )


def edge_tables(extended):
    cell_count = extended.shape[2] - 4
    centre = extended[:, :, 2 : 2 + cell_count]
    left_edge = wide_weight * (extended[:, :, 1 : 1 + cell_count] + centre) - narrow_weight * (
        extended[:, :, 0:cell_count] + extended[:, :, 3 : 3 + cell_count]
    )
    right_edge = wide_weight * (centre + extended[:, :, 3 : 3 + cell_count]) - narrow_weight * (
        extended[:, :, 1 : 1 + cell_count] + extended[:, :, 4 : 4 + cell_count]
    )
    edge_jump = right_edge - left_edge
    curvature = 6.0 * (centre - 0.5 * (left_edge + right_edge))
    return (right_edge, edge_jump, curvature)


def block_tables(block):
    depth, row_total, width_padded = block.shape
    cell_count = width_padded - 4
    right_edge, edge_jump, curvature = edge_tables(block)
    inner_cells = block[:, :, 2 : 2 + cell_count]
    earlier = lax.broadcasted_iota(jnp.int32, (cell_count, cell_count), 0)
    later = lax.broadcasted_iota(jnp.int32, (cell_count, cell_count), 1)
    strictly_before = (earlier < later).astype(jnp.float32)
    prefix = jnp.dot(
        inner_cells.reshape(depth * row_total, cell_count),
        strictly_before,
        precision=lax.Precision.HIGHEST,
    ).reshape(depth, row_total, cell_count)
    return jnp.stack((prefix, right_edge, edge_jump, curvature))


def rebase(table, subtract):
    return jnp.concatenate([(table[0] - subtract[:, :, None])[None], table[1:]], axis=0)


def on_device(tracers, offsets, fraction, courant_north):
    tracer_count, level_count, row_count, cells_dev = tracers.shape
    stack_depth = tracer_count * level_count
    field = tracers.reshape(stack_depth, row_count, cells_dev)
    rim_width = 2
    padded = with_halo(field, (("lon", 2),), rim_width, True)
    own_table = block_tables(padded)
    block_total = jnp.sum(field, axis=2)
    got_one, total_one = shifted((own_table, block_total), "lon", 1)
    got_two, total_two = shifted((own_table, block_total), "lon", 2)
    west_one = rebase(got_one, total_one)
    west_two = rebase(got_two, total_one + total_two)
    face_index = lax.broadcasted_iota(jnp.int32, (row_count, cells_dev), 1)
    source_index = face_index - offsets + 2 * cells_dev
    joined_width = 3 * cells_dev
    joined = jnp.concatenate([west_two, west_one, own_table], axis=3)
    block_rows = 8

    def lookup_block(block_turn, picked):
        first_row = block_turn * block_rows
        table_block = lax.dynamic_slice_in_dim(joined, first_row, block_rows, 2)
        source_block = lax.dynamic_slice_in_dim(source_index, first_row, block_rows, 0)
        column = lax.broadcasted_iota(jnp.int32, (block_rows, joined_width, cells_dev), 1)
        pick_source = (column == source_block[:, None, :]).astype(jnp.float32)
        pick_depart = (column == source_block[:, None, :] - 1).astype(jnp.float32)
        base_part = jnp.einsum(
            "drk,rkg->drg", table_block[0], pick_source, precision=lax.Precision.HIGHEST
        )
        other_parts = jnp.einsum(
            "tdrk,rkg->tdrg", table_block[1:], pick_depart, precision=lax.Precision.HIGHEST
        )
        result_block = jnp.concatenate([base_part[None], other_parts], axis=0)
        return lax.dynamic_update_slice_in_dim(picked, result_block, first_row, 2)

    picked = lax.fori_loop(
        0,
        row_count // block_rows,
        lookup_block,
        jnp.zeros((4, stack_depth, row_count, cells_dev), jnp.float32),
    )
    base_value = picked[0]
    zonal_flux = (
        own_table[0] - base_value + frac_flux(fraction[None], picked[1], picked[2], picked[3])
    )
    east_flux = shifted(zonal_flux[:, :, 0], "lon", -1)
    next_flux = jnp.concatenate([zonal_flux[:, :, 1:], east_flux[:, :, None]], axis=2)
    after_zonal = field - (next_flux - zonal_flux)
    combined = jnp.concatenate([after_zonal, courant_north[None]], axis=0)
    extended = with_halo(combined, (("lat", 1),), 3, False)
    merid_field = extended[:stack_depth]
    merid_courant = extended[stack_depth]

    def row_window(shift_by):
        return merid_field[:, 2 + shift_by : 3 + shift_by + row_count]

    merid_left = wide_weight * (row_window(-1) + row_window(0)) - narrow_weight * (
        row_window(-2) + row_window(1)
    )
    merid_right = wide_weight * (row_window(0) + row_window(1)) - narrow_weight * (
        row_window(-1) + row_window(2)
    )
    merid_jump = merid_right - merid_left
    merid_curve = 6.0 * (row_window(0) - 0.5 * (merid_left + merid_right))
    global_face = lax.axis_index("lat") * row_count + lax.broadcasted_iota(
        jnp.int32, (row_count + 1, cells_dev), 0
    )
    courant = jnp.where(global_face == 0, jnp.float32(0.0), merid_courant[3 : 4 + row_count])
    merid_flux = frac_flux(courant[None], merid_right, merid_jump, merid_curve)
    advected = after_zonal - (merid_flux[:, 1:] - merid_flux[:, :-1])
    return advected.reshape(tracer_count, level_count, row_count, cells_dev)


def solution(mesh):
    placed = (P(None, None, "lat", "lon"), P("lat", "lon"), P("lat", "lon"), P("lat", "lon"))
    return jax.shard_map(
        on_device,
        mesh=mesh,
        in_specs=placed,
        out_specs=P(None, None, "lat", "lon"),
        check_vma=False,
    )
```

profile of v0, /device:TPU:30, one launch (start us, length us, event | category | flops | bytes accessed | tf_op | source)
XLA Modules:
  0.0 145.6 jit_solution(6431882662171284448)
XLA Ops:
  0.0 1.2 copy.50
  1.2 2.7 %collective-permute-start = (f32[5,96,2]{1,0,2:T(8,128)S(1)}, f32[5,96,2]{1,0,2:T(8,128)S(1)}, u32[]{:S(2)}, u32[]{:S(2)}) collective-permute-start(f32[5,96,2]{1,0,2:T(8,128)S(1)} %get-tuple-element.152), channel_id=1, source_target_pairs={{1,0},{2,1},{3,2},{4,3},{5,4},{6,5},{7,6},{8,7},{9,8},{10,9},{11,1... | collective-permute-start | bytes 11528 | tf_op jit(solution)/shard_map/ppermute | solution.py:20
  3.9 4.0 %collective-permute-start.1 = (f32[5,96,2]{1,0,2:T(8,128)S(1)}, f32[5,96,2]{1,0,2:T(8,128)S(1)}, u32[]{:S(2)}, u32[]{:S(2)}) collective-permute-start(f32[5,96,2]{1,0,2:T(8,128)S(1)} %get-tuple-element.151), channel_id=1, source_target_pairs={{0,1},{1,2},{2,3},{3,4},{4,5},{5,6},{6,7},{7,8},{8,9},{9,10},{10,1... | collective-permute-start | bytes 11528 | tf_op jit(solution)/shard_map/ppermute | solution.py:17
  8.0 1.2 fusion.33
  9.2 8.0 %collective-permute-done.1 = f32[5,96,2]{1,0,2:T(8,128)S(1)} collective-permute-done((f32[5,96,2]{1,0,2:T(8,128)S(1)}, f32[5,96,2]{1,0,2:T(8,128)S(1)}, u32[]{:S(2)}, u32[]{:S(2)}) %collective-permute-start.1) | collective-permute-done | bytes 3872 | tf_op jit(solution)/shard_map/ppermute | solution.py:17
  18.1 1.9 %collective-permute-start.5 = (f32[4,5,96,128]{3,2,1,0:T(8,128)S(1)}, f32[4,5,96,128]{3,2,1,0:T(8,128)}, u32[]{:S(2)}, u32[]{:S(2)}) collective-permute-start(f32[4,5,96,128]{3,2,1,0:T(8,128)S(1)} %pad_maximum_fusion), channel_id=1, source_target_pairs={{0,1},{1,2},{2,3},{3,4},{4,5},{5,6},{6,7},{7,8},{8,9},{9,10},{10,1... | collective-permute-start | bytes 2949128 | tf_op jit(solution)/shard_map/ppermute | solution.py:28
  20.1 1.9 %collective-permute-start.2 = (f32[4,5,96,128]{3,2,1,0:T(8,128)S(1)}, f32[4,5,96,128]{3,2,1,0:T(8,128)}, u32[]{:S(2)}, u32[]{:S(2)}) collective-permute-start(f32[4,5,96,128]{3,2,1,0:T(8,128)S(1)} %pad_maximum_fusion), channel_id=1, source_target_pairs={{0,2},{1,3},{2,4},{3,5},{4,6},{5,7},{6,8},{7,9},{8,10},{9,11},{10,... | collective-permute-start | bytes 2949128 | tf_op jit(solution)/shard_map/ppermute | solution.py:28
  22.2 1.9 %collective-permute-start.3 = (f32[5,96]{1,0:T(8,128)S(1)}, f32[5,96]{1,0:T(8,128)S(1)}, u32[]{:S(2)}, u32[]{:S(2)}) collective-permute-start(f32[5,96]{1,0:T(8,128)S(1)} %reduce_sum.9), channel_id=1, source_target_pairs={{0,1},{1,2},{2,3},{3,4},{4,5},{5,6},{6,7},{7,8},{8,9},{9,10},{10,1... | collective-permute-start | bytes 5768 | tf_op jit(solution)/shard_map/ppermute | solution.py:28
  24.1 3.8 %collective-permute-start.4 = (f32[5,96]{1,0:T(8,128)S(1)}, f32[5,96]{1,0:T(8,128)S(1)}, u32[]{:S(2)}, u32[]{:S(2)}) collective-permute-start(f32[5,96]{1,0:T(8,128)S(1)} %reduce_sum.9), channel_id=1, source_target_pairs={{0,2},{1,3},{2,4},{3,5},{4,6},{5,7},{6,8},{7,9},{8,10},{9,11},{10,... | collective-permute-start | bytes 5768 | tf_op jit(solution)/shard_map/ppermute | solution.py:28
  28.1 1.0 copy.56
  29.3 32.1 %collective-permute-done.3 = f32[5,96]{1,0:T(8,128)S(1)} collective-permute-done((f32[5,96]{1,0:T(8,128)S(1)}, f32[5,96]{1,0:T(8,128)S(1)}, u32[]{:S(2)}, u32[]{:S(2)}) %collective-permute-start.3) | collective-permute-done | bytes 1952 | tf_op jit(solution)/shard_map/ppermute | solution.py:28
  61.4 6.7 %collective-permute-done.4 = f32[5,96]{1,0:T(8,128)S(1)} collective-permute-done((f32[5,96]{1,0:T(8,128)S(1)}, f32[5,96]{1,0:T(8,128)S(1)}, u32[]{:S(2)}, u32[]{:S(2)}) %collective-permute-start.4) | collective-permute-done | bytes 1952 | tf_op jit(solution)/shard_map/ppermute | solution.py:28
  68.1 1.2 slice.158
  69.3 1.1 slice_subtract_fusion.1
  70.4 1.2 slice.156
  71.5 1.1 slice_subtract_fusion.2
  72.6 1.8 %maximum_maximum_fusion = f32[4,5,96,384]{3,2,1,0:T(8,128)} fusion(f32[1,5,96,128]{3,2,1,0:T(8,128)S(1)} %copy.53, f32[1,5,96,128]{3,2,1,0:T(8,128)S(1)} %copy.52, f32[1,5,96,128]{3,2,1,0:T(8,128)S(1)} %copy.51, f32[1,5,96,128]{3,2,1,0:T(8,128)S(1)} %bitcast.83, f32[3,5,96,128]{3,2,1,0:T(8,128)S(1)} %slice.158, ...), kind=kLoop, calls=%fused_computation.16 | loop fusion | flops 5160960 | bytes 5898240 | tf_op jit(solution)/shard_map/concatenate | solution.py:86
  74.6 39.1 %while.15 = (s32[]{:T(128)}, f32[4,5,96,128]{3,1,0,2:T(8,128)S(1)}, s32[96,128]{1,0:T(8,128)S(1)}, f32[4,5,96,384]{3,2,1,0:T(8,128)}, s32[]{:T(128)}, /*index=5*/s32[]{:T(128)}, s32[]{:T(128)}, s32[]{:T(128)}, s32[]{}) while((s32[]{:T(128)}, f32[4,5,96,128]{3,1,0,2:T(8,128)S(1)}, s32[96,128]{1,0:T(8,128)S(1)}, f32[4,5,96,384]{3,2,1,0:T(8,128)}, ...), condition=%wide.region_2.0_spmd, body=%wide.region_1.0_spmd.sunk | while | flops 95179784 | bytes 1101995 | solution.py:105
  74.6 0.9 constant_dynamic-slice_fusion.6
  75.6 0.7 fusion.44
  76.3 0.8 constant_dynamic-slice_fusion.7
  77.9 0.9 constant_dynamic-slice_fusion.6
  78.9 0.7 fusion.44
  79.6 0.8 constant_dynamic-slice_fusion.7
  81.2 0.9 constant_dynamic-slice_fusion.6
  82.1 0.7 fusion.44
  82.8 0.8 constant_dynamic-slice_fusion.7
  84.4 0.9 constant_dynamic-slice_fusion.6
  85.4 0.7 fusion.44
  86.1 0.8 constant_dynamic-slice_fusion.7
  87.7 0.9 constant_dynamic-slice_fusion.6
  88.6 0.7 fusion.44
  89.4 0.8 constant_dynamic-slice_fusion.7
  90.9 0.9 constant_dynamic-slice_fusion.6
  91.9 0.7 fusion.44
  92.6 0.8 constant_dynamic-slice_fusion.7
  94.2 0.9 constant_dynamic-slice_fusion.6
  95.2 0.7 fusion.44
  95.9 0.8 constant_dynamic-slice_fusion.7
  97.5 0.9 constant_dynamic-slice_fusion.6
  98.4 0.7 fusion.44
  99.1 0.8 constant_dynamic-slice_fusion.7
  100.7 0.9 constant_dynamic-slice_fusion.6
  101.7 0.7 fusion.44
  102.4 0.8 constant_dynamic-slice_fusion.7
  104.0 0.9 constant_dynamic-slice_fusion.6
  104.9 0.7 fusion.44
  105.7 0.8 constant_dynamic-slice_fusion.7
  107.2 0.9 constant_dynamic-slice_fusion.6
  108.2 0.7 fusion.44
  108.9 0.8 constant_dynamic-slice_fusion.7
  110.5 0.9 constant_dynamic-slice_fusion.6
  111.5 0.7 fusion.44
  112.2 0.8 constant_dynamic-slice_fusion.7
  113.7 1.2 copy-done
  114.9 2.1 %copy.55 = f32[4,5,96,128]{2,1,3,0:T(8,128)S(1)} copy(f32[4,5,96,128]{3,1,0,2:T(8,128)} %copy-done) | data formatting | bytes 1966080 | tf_op jit(solution)/shard_map/while | solution.py:105
  117.0 1.3 fusion.24
  118.3 3.3 %collective-permute-start.6 = (f32[5,96]{1,0:T(8,128)S(1)}, f32[5,96]{1,0:T(8,128)S(1)}, u32[]{:S(2)}, u32[]{:S(2)}) collective-permute-start(f32[5,96]{1,0:T(8,128)S(1)} %slice_bitcast_fusion.4), channel_id=1, source_target_pairs={{0,15},{1,0},{2,1},{3,2},{4,3},{5,4},{6,5},{7,6},{8,7},{9,8},{10,9... | collective-permute-start | bytes 5768 | tf_op jit(solution)/shard_map/ppermute | solution.py:28
  121.7 2.9 %collective-permute-done.6 = f32[5,96]{1,0:T(8,128)S(1)} collective-permute-done((f32[5,96]{1,0:T(8,128)S(1)}, f32[5,96]{1,0:T(8,128)S(1)}, u32[]{:S(2)}, u32[]{:S(2)}) %collective-permute-start.6) | collective-permute-done | bytes 1952 | tf_op jit(solution)/shard_map/ppermute | solution.py:28
  125.2 1.9 %collective-permute-start.7 = (f32[6,3,128]{1,0,2:T(8,128)S(1)}, f32[6,3,128]{1,0,2:T(8,128)S(1)}, u32[]{:S(2)}, u32[]{:S(2)}) collective-permute-start(f32[6,3,128]{1,0,2:T(8,128)S(1)} %get-tuple-element.150), channel_id=1, source_target_pairs={{16,0},{32,16},{48,32},{64,48},{80,64},{96,80},{112,96},{128,112},... | collective-permute-start | bytes 27656 | tf_op jit(solution)/shard_map/ppermute | solution.py:20
  127.1 2.4 %collective-permute-start.8 = (f32[6,3,128]{1,0,2:T(8,128)S(1)}, f32[6,3,128]{1,0,2:T(8,128)S(1)}, u32[]{:S(2)}, u32[]{:S(2)}) collective-permute-start(f32[6,3,128]{1,0,2:T(8,128)S(1)} %get-tuple-element.149), channel_id=1, source_target_pairs={{0,16},{16,32},{32,48},{48,64},{64,80},{80,96},{96,112},{112,128},... | collective-permute-start | bytes 27656 | tf_op jit(solution)/shard_map/ppermute | solution.py:17
  129.6 9.9 %collective-permute-done.7 = f32[6,3,128]{1,0,2:T(8,128)S(1)} collective-permute-done((f32[6,3,128]{1,0,2:T(8,128)S(1)}, f32[6,3,128]{1,0,2:T(8,128)S(1)}, u32[]{:S(2)}, u32[]{:S(2)}) %collective-permute-start.7) | collective-permute-done | bytes 9248 | tf_op jit(solution)/shard_map/ppermute | solution.py:20
  139.8 3.7 %collective-permute-done.8 = f32[6,3,128]{1,0,2:T(8,128)S(1)} collective-permute-done((f32[6,3,128]{1,0,2:T(8,128)S(1)}, f32[6,3,128]{1,0,2:T(8,128)S(1)}, u32[]{:S(2)}, u32[]{:S(2)}) %collective-permute-start.8) | collective-permute-done | bytes 9248 | tf_op jit(solution)/shard_map/ppermute | solution.py:17
  144.7 0.9 copy.64
  (74 shorter events, 12.3 us)
Async XLA Ops:
  1.2 8.0 %collective-permute-start = (f32[5,96,2]{1,0,2:T(8,128)S(1)}, f32[5,96,2]{1,0,2:T(8,128)S(1)}, u32[]{:S(2)}, u32[]{:S(2)}) collective-permute-start(f32[5,96,2]{1,0,2:T(8,128)S(1)} %get-tuple-element.152), channel_id=1, source_target_pairs={{1,0},{2,1},{3,2},{4,3},{5,4},{6,5},{7,6},{8,7},{9,8},{10,9},{11,1... | collective-permute-start | bytes 11528 | tf_op jit(solution)/shard_map/ppermute | solution.py:20
  3.9 13.2 %collective-permute-start.1 = (f32[5,96,2]{1,0,2:T(8,128)S(1)}, f32[5,96,2]{1,0,2:T(8,128)S(1)}, u32[]{:S(2)}, u32[]{:S(2)}) collective-permute-start(f32[5,96,2]{1,0,2:T(8,128)S(1)} %get-tuple-element.151), channel_id=1, source_target_pairs={{0,1},{1,2},{2,3},{3,4},{4,5},{5,6},{6,7},{7,8},{8,9},{9,10},{10,1... | collective-permute-start | bytes 11528 | tf_op jit(solution)/shard_map/ppermute | solution.py:17
  17.3 4.6 %copy-start.1 = (f32[5,1,96,128]{3,2,1,0:T(8,128)S(1)}, f32[5,1,96,128]{3,2,1,0:T(8,128)}, u32[]{:S(2)}) copy-start(f32[5,1,96,128]{3,2,1,0:T(8,128)} %param.6) | copy-start | bytes 737284
  17.4 10.6 %copy-start.2 = (f32[96,128]{1,0:T(8,128)S(1)}, f32[96,128]{1,0:T(8,128)}, u32[]{:S(2)}) copy-start(f32[96,128]{1,0:T(8,128)} %param.8) | copy-start | bytes 147460
  17.4 10.6 %copy-start.4 = (s32[96,128]{1,0:T(8,128)S(1)}, s32[96,128]{1,0:T(8,128)}, u32[]{:S(2)}) copy-start(s32[96,128]{1,0:T(8,128)} %param.7) | copy-start | bytes 147460
  18.1 50.0 %collective-permute-start.5 = (f32[4,5,96,128]{3,2,1,0:T(8,128)S(1)}, f32[4,5,96,128]{3,2,1,0:T(8,128)}, u32[]{:S(2)}, u32[]{:S(2)}) collective-permute-start(f32[4,5,96,128]{3,2,1,0:T(8,128)S(1)} %pad_maximum_fusion), channel_id=1, source_target_pairs={{0,1},{1,2},{2,3},{3,4},{4,5},{5,6},{6,7},{7,8},{8,9},{9,10},{10,1... | collective-permute-start | bytes 2949128 | tf_op jit(solution)/shard_map/ppermute | solution.py:28
  20.1 50.3 %collective-permute-start.2 = (f32[4,5,96,128]{3,2,1,0:T(8,128)S(1)}, f32[4,5,96,128]{3,2,1,0:T(8,128)}, u32[]{:S(2)}, u32[]{:S(2)}) collective-permute-start(f32[4,5,96,128]{3,2,1,0:T(8,128)S(1)} %pad_maximum_fusion), channel_id=1, source_target_pairs={{0,2},{1,3},{2,4},{3,5},{4,6},{5,7},{6,8},{7,9},{8,10},{9,11},{10,... | collective-permute-start | bytes 2949128 | tf_op jit(solution)/shard_map/ppermute | solution.py:28
  22.2 39.2 %collective-permute-start.3 = (f32[5,96]{1,0:T(8,128)S(1)}, f32[5,96]{1,0:T(8,128)S(1)}, u32[]{:S(2)}, u32[]{:S(2)}) collective-permute-start(f32[5,96]{1,0:T(8,128)S(1)} %reduce_sum.9), channel_id=1, source_target_pairs={{0,1},{1,2},{2,3},{3,4},{4,5},{5,6},{6,7},{7,8},{8,9},{9,10},{10,1... | collective-permute-start | bytes 5768 | tf_op jit(solution)/shard_map/ppermute | solution.py:28
  24.1 44.0 %collective-permute-start.4 = (f32[5,96]{1,0:T(8,128)S(1)}, f32[5,96]{1,0:T(8,128)S(1)}, u32[]{:S(2)}, u32[]{:S(2)}) collective-permute-start(f32[5,96]{1,0:T(8,128)S(1)} %reduce_sum.9), channel_id=1, source_target_pairs={{0,2},{1,3},{2,4},{3,5},{4,6},{5,7},{6,8},{7,9},{8,10},{9,11},{10,... | collective-permute-start | bytes 5768 | tf_op jit(solution)/shard_map/ppermute | solution.py:28
  113.7 1.2 copy-start
  114.9 6.7 %copy-start.3 = (f32[96,128]{1,0:T(8,128)S(1)}, f32[96,128]{1,0:T(8,128)}, u32[]{:S(2)}) copy-start(f32[96,128]{1,0:T(8,128)} %param.9) | copy-start | bytes 147460
  118.3 6.4 %collective-permute-start.6 = (f32[5,96]{1,0:T(8,128)S(1)}, f32[5,96]{1,0:T(8,128)S(1)}, u32[]{:S(2)}, u32[]{:S(2)}) collective-permute-start(f32[5,96]{1,0:T(8,128)S(1)} %slice_bitcast_fusion.4), channel_id=1, source_target_pairs={{0,15},{1,0},{2,1},{3,2},{4,3},{5,4},{6,5},{7,6},{8,7},{9,8},{10,9... | collective-permute-start | bytes 5768 | tf_op jit(solution)/shard_map/ppermute | solution.py:28
  125.2 14.2 %collective-permute-start.7 = (f32[6,3,128]{1,0,2:T(8,128)S(1)}, f32[6,3,128]{1,0,2:T(8,128)S(1)}, u32[]{:S(2)}, u32[]{:S(2)}) collective-permute-start(f32[6,3,128]{1,0,2:T(8,128)S(1)} %get-tuple-element.150), channel_id=1, source_target_pairs={{16,0},{32,16},{48,32},{64,48},{80,64},{96,80},{112,96},{128,112},... | collective-permute-start | bytes 27656 | tf_op jit(solution)/shard_map/ppermute | solution.py:20
  127.1 16.4 %collective-permute-start.8 = (f32[6,3,128]{1,0,2:T(8,128)S(1)}, f32[6,3,128]{1,0,2:T(8,128)S(1)}, u32[]{:S(2)}, u32[]{:S(2)}) collective-permute-start(f32[6,3,128]{1,0,2:T(8,128)S(1)} %get-tuple-element.149), channel_id=1, source_target_pairs={{0,16},{16,32},{32,48},{48,64},{64,80},{80,96},{96,112},{112,128},... | collective-permute-start | bytes 27656 | tf_op jit(solution)/shard_map/ppermute | solution.py:17
where the time goes:
time: 147 us; the launch traced here: 146 us
  waiting for transfers between devices  63.3 us (43%)
  local copies, waits for them, and re-layouts  31.2 us (21%)
  starting transfers between devices  24 us (16%)
  matrix products  17.9 us (12%)
  other arithmetic  8.29 us (6%)
    ppermute x5, waiting for transfers between devices, shifted(): return lax.ppermute(value, axis, pairs)  41.8 us
    ppermute x5, starting transfers between devices, shifted(): return lax.ppermute(value, axis, pairs)  12.9 us
    ppermute x2, waiting for transfers between devices, with_halo(): lax.ppermute(lax.slice_in_dim(block, block.shape[dim] - width, None, axis...  11.7 us
    slice x12, local copies, waits for them, and re-layouts, lookup_block(): table_block[1:]  11.3 us
    slice x12, local copies, waits for them, and re-layouts, lookup_block(): table_block[0]  10.1 us
    ppermute x2, waiting for transfers between devices, with_halo(): lax.ppermute(lax.slice_in_dim(block, 0, width, axis=dim), axis, backward)  9.87 us
    dot_general x12, matrix products, lookup_block(): jnp.einsum('tdrk,rkg->tdrg', table_block[1:], pick_depart, precision=lax....  8.63 us
    dot_general x12, matrix products, lookup_block(): jnp.einsum('drk,rkg->drg', table_block[0], pick_source, precision=lax.Pre...  8.08 us
  transfers between devices with their start and end apart: 9, of which 6 were waited for; matrix products, arithmetic and copies ran while one was open for 4% of the time, Pallas kernels for 0%

commit v1 on v0

v1 whole, which is shorter than its diff:
```python
import functools

import jax
import jax.numpy as jnp
from jax import lax
from jax.experimental import pallas as pl
from jax.experimental.pallas import tpu as pltpu
from jax.sharding import PartitionSpec as P

wide_weight = 7.0 / 12.0
narrow_weight = 1.0 / 12.0
MESH = pl.DeviceIdType.MESH
SUB = 8
RIM = 16
POLAR_GROUPS = 3
FULL_GROUPS = 6


def take(table, index):
    return jnp.take_along_axis(table, index, axis=1, mode="promise_in_bounds")


def split_dot(value, matrix):
    high = value.astype(jnp.bfloat16)
    low = (value - high.astype(jnp.float32)).astype(jnp.bfloat16)
    return jnp.dot(high, matrix, preferred_element_type=jnp.float32) + jnp.dot(
        low, matrix, preferred_element_type=jnp.float32
    )


def frac_flux(courant, right, left, centre):
    jump = right - left
    curve = 6.0 * (centre - 0.5 * (left + right))
    return courant * (right - 0.5 * courant * (jump - (1.0 - 2.0 / 3.0 * courant) * curve))


def roll(value, steps):
    steps = steps % value.shape[-1]
    return value if steps == 0 else pltpu.roll(value, steps, 1)


def edge_pair(cells, west, east, lane):
    last = cells.shape[-1]
    minus_two = roll(jnp.where(lane >= last - 2, west, cells), 2)
    minus_one = roll(jnp.where(lane >= last - 1, west, cells), 1)
    plus_one = roll(jnp.where(lane < 1, east, cells), -1)
    plus_two = roll(jnp.where(lane < 2, east, cells), -2)
    left = wide_weight * (minus_one + cells) - narrow_weight * (minus_two + plus_one)
    right = wide_weight * (cells + plus_one) - narrow_weight * (minus_one + plus_two)
    return left, right


def kernel(
    sizes, tr, off_in, fr_in, cn_in, out,
    buf, off_buf, fr_buf, cn_buf, west_two, pack, ecol, got_pack, got_ecol, got_far,
    lo_buf, prefix, total, suffix, after, edge_buf, flux_buf,
    local_sem, send_sem, recv_sem,
):
    lat_count, lon_count = sizes
    depth, rows, lanes = tr.shape
    groups = rows // SUB
    slots = lanes // RIM
    lat, lon = lax.axis_index("lat"), lax.axis_index("lon")
    south_end = lat == 0
    north_end = lat == lat_count - 1
    polar = south_end | north_end

    local = [
        pltpu.make_async_copy(tr, buf.at[0], local_sem.at[0]),
        pltpu.make_async_copy(off_in, off_buf, local_sem.at[1]),
        pltpu.make_async_copy(fr_in, fr_buf, local_sem.at[2]),
        pltpu.make_async_copy(cn_in, cn_buf.at[pl.ds(0, rows)], local_sem.at[3]),
    ]
    for copy in local:
        copy.start()

    def lon_dev(steps):
        return {"lat": lat, "lon": lax.rem(lon + steps + lon_count, lon_count)}

    def lat_dev(steps):
        return {"lat": lax.rem(lat + steps + lat_count, lat_count), "lon": lon}

    barrier = pltpu.get_barrier_semaphore()
    for device in (lon_dev(1), lon_dev(-1), lat_dev(1), lat_dev(-1)):
        pl.semaphore_signal(barrier, inc=1, device_id=device, device_id_type=MESH)

    @pl.when(polar)
    def _():
        for steps in (2, -2, 3, -3):
            pl.semaphore_signal(barrier, inc=1, device_id=lon_dev(steps), device_id_type=MESH)

    lane = lax.broadcasted_iota(jnp.int32, (SUB, lanes), 1)
    slot_of = lane // RIM

    for copy in local[:3]:
        copy.wait()

    for tile in range(-(-depth * groups // slots)):
        packed = jnp.zeros((SUB, lanes), jnp.float32)
        for slot in range(slots):
            group, t = divmod(tile * slots + slot, depth)
            if group >= groups:
                break
            cells = buf[0, t, group * SUB : (group + 1) * SUB, :]
            packed = jnp.where(slot_of == slot, roll(cells, RIM * (slot + 1)), packed)
        pack[tile] = packed
    for tile in range(ecol.shape[0]):
        packed = jnp.zeros((SUB, lanes), jnp.float32)
        for slot in range(slots):
            group = tile * slots + slot
            if group >= groups:
                break
            span = slice(group * SUB, (group + 1) * SUB)
            base = slot * RIM
            for t in range(depth):
                at = base + 2 * t
                packed = jnp.where((lane >= at) & (lane < at + 2), roll(buf[0, t, span, :], at), packed)
            at = base + 2 * depth
            packed = jnp.where(lane == at, roll(off_buf[span, :].astype(jnp.float32), at), packed)
            packed = jnp.where(lane == at + 1, roll(fr_buf[span, :], at + 1), packed)
        ecol[tile] = packed

    pl.semaphore_wait(barrier, jnp.where(polar, 8, 4))

    def remote(source, target, index, device):
        return pltpu.make_async_remote_copy(
            src_ref=source, dst_ref=target, send_sem=send_sem.at[index], recv_sem=recv_sem.at[index],
            device_id=device, device_id_type=MESH,
        )

    full_row = jnp.where(south_end, 0, rows - FULL_GROUPS * SUB)
    full_span = pl.ds(pl.multiple_of(full_row, SUB), FULL_GROUPS * SUB)
    polar_row = jnp.where(south_end, 0, rows - POLAR_GROUPS * SUB)
    polar_span = pl.ds(pl.multiple_of(polar_row, SUB), POLAR_GROUPS * SUB)
    far_span = pl.ds(jnp.where(south_end, 0, pack.shape[0] - 3), 3)
    polar_copies = [
        remote(tr.at[:, full_span], buf.at[1, :, full_span], 3, lon_dev(1)),
        remote(tr.at[:, polar_span], west_two.at[:, polar_span], 4, lon_dev(2)),
        remote(pack.at[far_span], got_far.at[far_span], 5, lon_dev(3)),
    ]

    @pl.when(polar)
    def _():
        for copy in polar_copies:
            copy.start()

    rim_copies = [
        remote(pack, got_pack, 0, lon_dev(1)),
        remote(ecol, got_ecol, 1, lon_dev(-1)),
        remote(cn_in.at[pl.ds(0, SUB)], cn_buf.at[pl.ds(rows, SUB)], 2, lat_dev(-1)),
    ]
    for copy in rim_copies:
        copy.start()

    row_of = lax.broadcasted_iota(jnp.int32, (lanes, lanes), 0)
    col_of = lax.broadcasted_iota(jnp.int32, (lanes, lanes), 1)
    ones = jnp.ones((lanes, lanes), jnp.float32)
    upto = (row_of <= col_of).astype(jnp.float32)
    prefix_matrix = jnp.concatenate([upto, ones], axis=1).astype(jnp.bfloat16)
    suffix_matrix = (upto - ones).astype(jnp.bfloat16)

    def prefix_of(which, t):
        both = split_dot(buf[which, t], prefix_matrix)
        prefix[which, t] = both[:, :lanes]
        total[which, t] = both[:, lanes:]

    for t in range(depth):
        prefix_of(0, t)
    local[3].wait()

    for copy in rim_copies[:2]:
        copy.wait()

    @pl.when(polar)
    def _():
        for copy in polar_copies:
            copy.wait()
        for t in range(depth):
            prefix_of(1, t)

    def is_polar(group):
        return (south_end & (group < POLAR_GROUPS)) | (north_end & (group >= groups - POLAR_GROUPS))

    def is_full(group):
        return (south_end & (group < FULL_GROUPS)) | (north_end & (group >= groups - FULL_GROUPS))

    for tile in range(-(-depth * groups // slots)):
        packed = got_pack[tile]
        for slot in range(slots):
            group, t = divmod(tile * slots + slot, depth)
            if group >= groups:
                break
            span = slice(group * SUB, (group + 1) * SUB)
            lo_buf[t, span, :] = jnp.where(lane >= lanes - RIM, roll(packed, -RIM * (slot + 1)), 0.0)

    @pl.when(polar)
    def _():
        lo_buf[:, full_span, :] = buf[1, :, full_span, :]
        lo_buf[:, polar_span, :] = west_two[:, polar_span, :]

    for t in range(depth):
        suffix[t] = split_dot(lo_buf[t], suffix_matrix)

    def zonal(group):
        first = pl.multiple_of(group * SUB, SUB)
        span = pl.ds(first, SUB)
        far = jnp.where(is_polar(group), 1, 0)
        off = off_buf[span, :]
        courant = fr_buf[span, :]
        east = got_ecol[group // slots]
        base = lax.rem(group, slots) * RIM
        east_off = take(east, jnp.full((SUB, lanes), 0, jnp.int32) + (base + 2 * depth)).astype(jnp.int32)
        east_courant = take(east, jnp.full((SUB, lanes), 0, jnp.int32) + (base + 2 * depth + 1))
        depart = lane - off - 1 + far * lanes
        in_lo = depart < 0
        index = depart & (lanes - 1)
        east_index = (lanes - 1 - east_off + far * lanes) & (lanes - 1)
        for t in range(depth):
            own = buf[0, t, span, :]
            near = buf[far, t, span, :]
            low = lo_buf[t, span, :]
            order = group * depth + t
            beyond = take(got_far[order // slots], (lane + RIM * (lax.rem(order, slots) + 1)) & (lanes - 1))
            ahead = take(east, (lane + (base + 2 * t)) & (lanes - 1))
            ahead = jnp.where(far == 1, own, ahead)
            near_left, near_right = edge_pair(near, low, ahead, lane)
            low_left, low_right = edge_pair(low, beyond, near, lane)
            near_prefix = prefix[far, t, span, :]
            far_total = jnp.where(far == 1, total[far, t, span, :], 0.0)

            def pick(near_table, low_table):
                return jnp.where(in_lo, take(low_table, index), take(near_table, index))

            flux = (
                (prefix[0, t, span, :] - own + far_total)
                - pick(near_prefix, suffix[t, span, :])
                + frac_flux(courant, pick(near_right, low_right), pick(near_left, low_left), pick(near, low))
            )
            east_flux = (
                (total[0, t, span, :] + far_total)
                - take(near_prefix, east_index)
                + frac_flux(
                    east_courant, take(near_right, east_index), take(near_left, east_index), take(near, east_index)
                )
            )
            next_flux = roll(jnp.where(lane == 0, east_flux, flux), -1)
            after[t, pl.ds(pl.multiple_of(first + SUB, SUB), SUB), :] = own - (next_flux - flux)

    def edge_group(i, carry):
        zonal(i * (groups - 1))
        return carry

    lax.fori_loop(0, 2, edge_group, 0)
    lat_copies = [
        remote(after.at[:, pl.ds(SUB, SUB)], after.at[:, pl.ds(SUB + rows, SUB)], 6, lat_dev(-1)),
        remote(after.at[:, pl.ds(rows, SUB)], after.at[:, pl.ds(0, SUB)], 7, lat_dev(1)),
    ]
    for copy in lat_copies:
        copy.start()

    def inner_group(i, carry):
        zonal(i)
        return carry

    lax.fori_loop(1, groups - 1, inner_group, 0)
    rim_copies[2].wait()
    for copy in lat_copies:
        copy.wait()

    @pl.when(south_end)
    def _():
        after[:, 0:SUB, :] = jnp.zeros((depth, SUB, lanes), jnp.float32)
        cn_buf[0:1, :] = jnp.zeros((1, lanes), jnp.float32)

    @pl.when(north_end)
    def _():
        after[:, SUB + rows :, :] = jnp.zeros((depth, SUB, lanes), jnp.float32)
        cn_buf[rows:, :] = jnp.zeros((SUB, lanes), jnp.float32)

    courant = cn_buf[0 : rows + 1, :]
    for t in range(depth):
        edge_buf[t, 0 : rows + 2, :] = wide_weight * (
            after[t, SUB - 2 : SUB + rows, :] + after[t, SUB - 1 : SUB + rows + 1, :]
        ) - narrow_weight * (after[t, SUB - 3 : SUB + rows - 1, :] + after[t, SUB : SUB + rows + 2, :])
        flux_buf[t, 0 : rows + 1, :] = frac_flux(
            courant,
            edge_buf[t, 1 : rows + 2, :],
            edge_buf[t, 0 : rows + 1, :],
            after[t, SUB - 1 : SUB + rows, :],
        )
        out[t] = after[t, SUB : SUB + rows, :] - (flux_buf[t, 1 : rows + 1, :] - flux_buf[t, 0:rows, :])


def on_device(sizes, tracers, offsets, fraction, courant_north):
    tracer_count, level_count, rows, lanes = tracers.shape
    depth = tracer_count * level_count
    f32 = jnp.float32
    groups = rows // SUB
    slots = lanes // RIM
    advected = pl.pallas_call(
        functools.partial(kernel, sizes),
        out_shape=jax.ShapeDtypeStruct((depth, rows, lanes), f32),
        in_specs=[pl.BlockSpec(memory_space=pl.ANY)] * 4,
        out_specs=pl.BlockSpec(memory_space=pltpu.VMEM),
        scratch_shapes=[
            pltpu.VMEM((2, depth, rows, lanes), f32),
            pltpu.VMEM((rows, lanes), jnp.int32),
            pltpu.VMEM((rows, lanes), f32),
            pltpu.VMEM((rows + SUB, lanes), f32),
            pltpu.VMEM((depth, rows, lanes), f32),
            pltpu.VMEM((-(-depth * groups // slots), SUB, lanes), f32),
            pltpu.VMEM((-(-groups // slots), SUB, lanes), f32),
            pltpu.VMEM((-(-depth * groups // slots), SUB, lanes), f32),
            pltpu.VMEM((-(-groups // slots), SUB, lanes), f32),
            pltpu.VMEM((-(-depth * groups // slots), SUB, lanes), f32),
            pltpu.VMEM((depth, rows, lanes), f32),
            pltpu.VMEM((2, depth, rows, lanes), f32),
            pltpu.VMEM((2, depth, rows, lanes), f32),
            pltpu.VMEM((depth, rows, lanes), f32),
            pltpu.VMEM((depth, rows + 2 * SUB, lanes), f32),
            pltpu.VMEM((depth, rows + SUB, lanes), f32),
            pltpu.VMEM((depth, rows + SUB, lanes), f32),
            pltpu.SemaphoreType.DMA((4,)),
            pltpu.SemaphoreType.DMA((8,)),
            pltpu.SemaphoreType.DMA((8,)),
        ],
        compiler_params=pltpu.CompilerParams(collective_id=0, has_side_effects=True),
    )(tracers.reshape(depth, rows, lanes), offsets, fraction, courant_north)
    return advected.reshape(tracers.shape)


def solution(mesh):
    placed = (P(None, None, "lat", "lon"), P("lat", "lon"), P("lat", "lon"), P("lat", "lon"))
    return jax.shard_map(
        functools.partial(on_device, (mesh.shape["lat"], mesh.shape["lon"])),
        mesh=mesh,
        in_specs=placed,
        out_specs=P(None, None, "lat", "lon"),
        check_vma=False,
    )
```

time: 147 us -> 26.1 us (0.18)
  the two profiles are of different devices: /device:TPU:30 before, /device:TPU:64 now
where the time goes in v1:
time: 26.1 us; the launch traced here: 26 us
  Pallas kernels  24.3 us (93%)
  local copies, waits for them, and re-layouts  1.65 us (6%)
    pallas_call x1, Pallas kernels, on_device(): pl.pallas_call(functools.partial(kernel, sizes), out_shape=jax.ShapeDtype...  24.3 us
    unnamed x1, local copies, waits for them, and re-layouts  1.65 us

profile of v1, /device:TPU:64, one launch (start us, length us, event | category | flops | bytes accessed | tf_op | source)
XLA Modules:
  0.0 26.0 jit_solution(6669842917151293075)
XLA Ops:
  0.0 24.3 %shard_map.46 = f32[5,96,128]{2,1,0:T(8,128)} custom-call(f32[5,96,128]{2,1,0:T(8,128)} %bitcast.5, s32[96,128]{1,0:T(8,128)} %off_in.1, f32[96,128]{1,0:T(8,128)} %fr_in.1, f32[96,128]{1,0:T(8,128)} %cn_in.1), custom_call_target="tpu_custom_call" | custom-call | tf_op jit(solution)/shard_map/pallas_call | solution.py:300
  24.3 1.7 %copy.7 = f32[5,1,96,128]{3,2,1,0:T(8,128)} copy(f32[5,1,96,128]{3,2,1,0:T(8,128)} %bitcast.4) | data formatting | bytes 491520

commit v2 on v1

v2 whole, which is shorter than its diff:
```python
import functools

import jax
import jax.numpy as jnp
from jax import lax
from jax.experimental import pallas as pl
from jax.experimental.pallas import tpu as pltpu
from jax.sharding import PartitionSpec as P

wide_weight = 7.0 / 12.0
narrow_weight = 1.0 / 12.0
MESH = pl.DeviceIdType.MESH
SUB = 8
RIM = 16
POLAR_GROUPS = 3
FULL_GROUPS = 6


def take(table, index):
    return jnp.take_along_axis(table, index, axis=1, mode="promise_in_bounds")


def split_dot(value, matrix):
    high = value.astype(jnp.bfloat16)
    low = (value - high.astype(jnp.float32)).astype(jnp.bfloat16)
    return jnp.dot(high, matrix, preferred_element_type=jnp.float32) + jnp.dot(
        low, matrix, preferred_element_type=jnp.float32
    )


def frac_flux(courant, right, left, centre):
    jump = right - left
    curve = 6.0 * (centre - 0.5 * (left + right))
    return courant * (right - 0.5 * courant * (jump - (1.0 - 2.0 / 3.0 * courant) * curve))


def roll(value, steps):
    steps = steps % value.shape[-1]
    return value if steps == 0 else pltpu.roll(value, steps, 1)


def edge_pair(cells, west, east, lane):
    last = cells.shape[-1]
    minus_two = roll(jnp.where(lane >= last - 2, west, cells), 2)
    minus_one = roll(jnp.where(lane >= last - 1, west, cells), 1)
    plus_one = roll(jnp.where(lane < 1, east, cells), -1)
    plus_two = roll(jnp.where(lane < 2, east, cells), -2)
    left = wide_weight * (minus_one + cells) - narrow_weight * (minus_two + plus_one)
    right = wide_weight * (cells + plus_one) - narrow_weight * (minus_one + plus_two)
    return left, right


def packed_edges(cells, ahead, in_slot):
    minus_one = roll(cells, 1)
    minus_two = roll(cells, 2)
    plus_one = roll(jnp.where(in_slot < 1, ahead, cells), -1)
    plus_two = roll(jnp.where(in_slot < 2, ahead, cells), -2)
    left = wide_weight * (minus_one + cells) - narrow_weight * (minus_two + plus_one)
    right = wide_weight * (cells + plus_one) - narrow_weight * (minus_one + plus_two)
    return left, right


def zonal_kernel(
    sizes, tr, off_in, fr_in, cn_in, after, cn_buf,
    buf, off_buf, fr_buf, west_two, pack, ecol, got_pack, got_ecol, got_far,
    lo_buf, prefix, total, suffix, own_head, halo, east_flux_buf, low_left, low_right, low_sum,
    local_sem, send_sem, recv_sem,
):
    lat_count, lon_count = sizes
    depth, rows, lanes = tr.shape
    groups = rows // SUB
    slots = lanes // RIM
    tiles = pack.shape[0]
    lat, lon = lax.axis_index("lat"), lax.axis_index("lon")
    south_end = lat == 0
    north_end = lat == lat_count - 1
    polar = south_end | north_end
    has_south = lat > 0
    has_north = lat < lat_count - 1

    local = [
        pltpu.make_async_copy(tr, buf.at[0], local_sem.at[0]),
        pltpu.make_async_copy(off_in, off_buf, local_sem.at[1]),
        pltpu.make_async_copy(fr_in, fr_buf, local_sem.at[2]),
        pltpu.make_async_copy(cn_in, cn_buf.at[pl.ds(0, rows)], local_sem.at[3]),
    ]
    for copy in local:
        copy.start()

    def lon_dev(steps):
        return {"lat": lat, "lon": lax.rem(lon + steps + lon_count, lon_count)}

    def lat_dev(steps):
        return {"lat": lax.rem(lat + steps + lat_count, lat_count), "lon": lon}

    barrier = pltpu.get_barrier_semaphore()

    def greet(device):
        pl.semaphore_signal(barrier, inc=1, device_id=device, device_id_type=MESH)

    greet(lon_dev(1))
    greet(lon_dev(-1))
    pl.when(has_south)(lambda: greet(lat_dev(-1)))
    pl.when(has_north)(lambda: greet(lat_dev(1)))

    @pl.when(polar)
    def _():
        for steps in (2, -2, 3, -3):
            greet(lon_dev(steps))

    lane = lax.broadcasted_iota(jnp.int32, (SUB, lanes), 1)
    slot_of = lane // RIM
    in_slot = lane & (RIM - 1)

    for copy in local[:3]:
        copy.wait()

    for tile in range(tiles):
        packed = jnp.zeros((SUB, lanes), jnp.float32)
        for slot in range(slots):
            group, t = divmod(tile * slots + slot, depth)
            if group >= groups:
                break
            cells = buf[0, t, group * SUB : (group + 1) * SUB, :]
            packed = jnp.where(slot_of == slot, roll(cells, RIM * (slot + 1)), packed)
        pack[tile] = packed
    for tile in range(ecol.shape[0]):
        packed = jnp.zeros((SUB, lanes), jnp.float32)
        for slot in range(slots):
            group = tile * slots + slot
            if group >= groups:
                break
            span = slice(group * SUB, (group + 1) * SUB)
            base = slot * RIM
            for t in range(depth):
                at = base + 2 * t
                packed = jnp.where((lane >= at) & (lane < at + 2), roll(buf[0, t, span, :], at), packed)
            at = base + 2 * depth
            packed = jnp.where(lane == at, roll(off_buf[span, :].astype(jnp.float32), at), packed)
            packed = jnp.where(lane == at + 1, roll(fr_buf[span, :], at + 1), packed)
        ecol[tile] = packed

    pl.semaphore_wait(barrier, jnp.where(polar, 7, 4))

    def remote(source, target, index, device):
        return pltpu.make_async_remote_copy(
            src_ref=source, dst_ref=target, send_sem=send_sem.at[index], recv_sem=recv_sem.at[index],
            device_id=device, device_id_type=MESH,
        )

    full_row = jnp.where(south_end, 0, rows - FULL_GROUPS * SUB)
    full_span = pl.ds(pl.multiple_of(full_row, SUB), FULL_GROUPS * SUB)
    polar_row = jnp.where(south_end, 0, rows - POLAR_GROUPS * SUB)
    polar_span = pl.ds(pl.multiple_of(polar_row, SUB), POLAR_GROUPS * SUB)
    far_span = pl.ds(jnp.where(south_end, 0, tiles - 3), 3)
    rim_copies = [
        remote(pack, got_pack, 0, lon_dev(1)),
        remote(ecol, got_ecol, 1, lon_dev(-1)),
    ]
    for copy in rim_copies:
        copy.start()
    polar_copies = [
        remote(tr.at[:, full_span], buf.at[1, :, full_span], 3, lon_dev(1)),
        remote(tr.at[:, polar_span], west_two.at[:, polar_span], 4, lon_dev(2)),
        remote(pack.at[far_span], got_far.at[far_span], 5, lon_dev(3)),
    ]

    @pl.when(polar)
    def _():
        for copy in polar_copies:
            copy.start()

    courant_copy = remote(cn_in.at[pl.ds(0, SUB)], cn_buf.at[pl.ds(rows, SUB)], 2, lat_dev(-1))
    pl.when(has_south)(courant_copy.start)

    row_of = lax.broadcasted_iota(jnp.int32, (lanes, lanes), 0)
    col_of = lax.broadcasted_iota(jnp.int32, (lanes, lanes), 1)
    ones = jnp.ones((lanes, lanes), jnp.float32)
    upto = (row_of <= col_of).astype(jnp.float32)
    prefix_matrix = jnp.concatenate([upto, ones], axis=1).astype(jnp.bfloat16)
    suffix_matrix = (upto - ones).astype(jnp.bfloat16)
    slot_matrix = jnp.where(row_of // RIM == col_of // RIM, upto - ones, 0.0).astype(jnp.bfloat16)

    for t in range(depth):
        both = split_dot(buf[0, t], prefix_matrix)
        prefix[0, t] = both[:, :lanes]
        total[0, t] = both[:, lanes:]
    tail_sum = split_dot(pack[...].reshape(tiles * SUB, lanes), slot_matrix)

    def slot_pattern(tile, turn):
        order = jnp.minimum(tile * slots + ((slot_of + turn) & (slots - 1)), depth * groups - 1)
        group = (order * 13) >> 6
        return (group & (slots - 1)) * RIM, order - depth * group

    def heads(columns, tile):
        base, t = slot_pattern(tile, slots - 1)
        return take(columns[tile * slots // (depth * slots)], base + 2 * t + (lane & 1))

    for tile in range(tiles):
        own_head[tile] = heads(ecol, tile)
    local[3].wait()

    for copy in rim_copies:
        copy.wait()

    got_sum = split_dot(got_pack[...].reshape(tiles * SUB, lanes), slot_matrix)
    for tile in range(tiles):
        base, t = slot_pattern(tile, 0)
        columns = got_ecol[tile * slots // (depth * slots)]
        ahead = heads(got_ecol, tile)
        tail = pack[tile]
        left, right = packed_edges(tail, ahead, in_slot)
        depart = take(columns, base + 2 * depth).astype(jnp.int32)
        courant = take(columns, base + 2 * depth + 1)
        index = (slot_of * RIM + (RIM - 1) - depart) & (lanes - 1)
        span = slice(tile * SUB, (tile + 1) * SUB)
        east_flux_buf[tile] = frac_flux(courant, take(right, index), take(left, index), take(tail, index)) - take(
            tail_sum[span], index
        )
        west = got_pack[tile]
        low_left[tile], low_right[tile] = packed_edges(west, own_head[tile], in_slot)
        low_sum[tile] = got_sum[span]
        halo[tile] = jnp.where(in_slot < 2, ahead, west)

    def finish(t, first, own, flux, east_flux):
        next_flux = roll(jnp.where(lane == 0, east_flux, flux), -1)
        after[t, pl.ds(pl.multiple_of(first + SUB, SUB), SUB), :] = own - (next_flux - flux)

    def near_zonal(group):
        first = pl.multiple_of(group * SUB, SUB)
        span = pl.ds(first, SUB)
        courant = fr_buf[span, :]
        depart = lane - off_buf[span, :] - 1
        in_low = depart < 0
        index = depart & (lanes - 1)
        for t in range(depth):
            order = group * depth + t
            tile, slot = order // slots, lax.rem(order, slots)
            own = buf[0, t, span, :]
            around = take(halo[tile], (lane + RIM * (slot + 1)) & (lanes - 1))
            left, right = edge_pair(own, around, around, lane)
            own_prefix = prefix[0, t, span, :]
            low_index = (depart + RIM * (slot + 1)) & (lanes - 1)

            def pick(table, low_table):
                return jnp.where(in_low, take(low_table[tile], low_index), take(table, index))

            flux = (
                (own_prefix - own)
                - pick(own_prefix, low_sum)
                + frac_flux(courant, pick(right, low_right), pick(left, low_left), pick(own, got_pack))
            )
            east_flux = take(east_flux_buf[tile], jnp.full((SUB, lanes), 0, jnp.int32) + slot * RIM)
            finish(t, first, own, flux, east_flux)

    def is_polar(group):
        return (south_end & (group < POLAR_GROUPS)) | (north_end & (group >= groups - POLAR_GROUPS))

    def full_zonal(group):
        first = pl.multiple_of(group * SUB, SUB)
        span = pl.ds(first, SUB)
        far = jnp.where(is_polar(group), 1, 0)
        off = off_buf[span, :]
        courant = fr_buf[span, :]
        east = got_ecol[group // slots]
        base = lax.rem(group, slots) * RIM
        east_off = take(east, jnp.full((SUB, lanes), 0, jnp.int32) + (base + 2 * depth)).astype(jnp.int32)
        east_courant = take(east, jnp.full((SUB, lanes), 0, jnp.int32) + (base + 2 * depth + 1))
        depart = lane - off - 1 + far * lanes
        in_low = depart < 0
        index = depart & (lanes - 1)
        east_index = (lanes - 1 - east_off + far * lanes) & (lanes - 1)
        for t in range(depth):
            own = buf[0, t, span, :]
            near = buf[far, t, span, :]
            low = lo_buf[t, span, :]
            order = group * depth + t
            beyond = take(got_far[order // slots], (lane + RIM * (lax.rem(order, slots) + 1)) & (lanes - 1))
            ahead = take(east, (lane + (base + 2 * t)) & (lanes - 1))
            ahead = jnp.where(far == 1, own, ahead)
            near_left, near_right = edge_pair(near, low, ahead, lane)
            far_left, far_right = edge_pair(low, beyond, near, lane)
            near_prefix = prefix[far, t, span, :]
            far_total = jnp.where(far == 1, total[far, t, span, :], 0.0)

            def pick(near_table, low_table):
                return jnp.where(in_low, take(low_table, index), take(near_table, index))

            flux = (
                (prefix[0, t, span, :] - own + far_total)
                - pick(near_prefix, suffix[t, span, :])
                + frac_flux(courant, pick(near_right, far_right), pick(near_left, far_left), pick(near, low))
            )
            east_flux = (
                (total[0, t, span, :] + far_total)
                - take(near_prefix, east_index)
                + frac_flux(
                    east_courant, take(near_right, east_index), take(near_left, east_index), take(near, east_index)
                )
            )
            finish(t, first, own, flux, east_flux)

    near_zonal(jnp.where(south_end, groups - 1, 0))
    near_zonal(jnp.where(north_end, 1, jnp.where(south_end, groups - 2, groups - 1)))
    to_south = remote(after.at[:, pl.ds(SUB, SUB)], after.at[:, pl.ds(SUB + rows, SUB)], 6, lat_dev(-1))
    to_north = remote(after.at[:, pl.ds(rows, SUB)], after.at[:, pl.ds(0, SUB)], 7, lat_dev(1))
    pl.when(has_south)(to_south.start)
    pl.when(has_north)(to_north.start)

    inner = jnp.where(south_end, FULL_GROUPS, jnp.where(north_end, 2, 1))
    pairs = jnp.where(polar, (groups - FULL_GROUPS) // 2 - 1, groups // 2 - 1)

    def inner_pair(i, carry):
        near_zonal(inner + 2 * i)
        near_zonal(inner + 2 * i + 1)
        return carry

    lax.fori_loop(0, pairs, inner_pair, 0)

    @pl.when(polar)
    def _():
        for copy in polar_copies:
            copy.wait()
        lo_buf[:, full_span, :] = buf[1, :, full_span, :]
        lo_buf[:, polar_span, :] = west_two[:, polar_span, :]
        for t in range(depth):
            both = split_dot(buf[1, t, polar_span, :], prefix_matrix)
            prefix[1, t, polar_span, :] = both[:, :lanes]
            total[1, t, polar_span, :] = both[:, lanes:]
            suffix[t, full_span, :] = split_dot(lo_buf[t, full_span, :], suffix_matrix)

        def full_pair(i, carry):
            full_zonal(full_row // SUB + 2 * i)
            full_zonal(full_row // SUB + 2 * i + 1)
            return carry

        lax.fori_loop(0, FULL_GROUPS // 2, full_pair, 0)

    @pl.when(has_south)
    def _():
        courant_copy.wait_send()
        to_south.wait_send()
        to_north.wait_recv()

    @pl.when(has_north)
    def _():
        to_north.wait_send()
        to_south.wait_recv()
        courant_copy.wait_recv()

    @pl.when(south_end)
    def _():
        after[:, 0:SUB, :] = jnp.zeros((depth, SUB, lanes), jnp.float32)
        cn_buf[0:1, :] = jnp.zeros((1, lanes), jnp.float32)

    @pl.when(north_end)
    def _():
        after[:, SUB + rows :, :] = jnp.zeros((depth, SUB, lanes), jnp.float32)
        cn_buf[rows:, :] = jnp.zeros((SUB, lanes), jnp.float32)


def merid_kernel(after, cn_buf, out, edge_buf, flux_buf, done, sems):
    depth, rows, lanes = out.shape
    courant = cn_buf[0 : rows + 1, :]
    copies = []
    for t in range(depth):
        edge_buf[t, 0 : rows + 2, :] = wide_weight * (
            after[t, SUB - 2 : SUB + rows, :] + after[t, SUB - 1 : SUB + rows + 1, :]
        ) - narrow_weight * (after[t, SUB - 3 : SUB + rows - 1, :] + after[t, SUB : SUB + rows + 2, :])
        flux_buf[t, 0 : rows + 1, :] = frac_flux(
            courant,
            edge_buf[t, 1 : rows + 2, :],
            edge_buf[t, 0 : rows + 1, :],
            after[t, SUB - 1 : SUB + rows, :],
        )
        done[t] = after[t, SUB : SUB + rows, :] - (flux_buf[t, 1 : rows + 1, :] - flux_buf[t, 0:rows, :])
        copies.append(pltpu.make_async_copy(done.at[t], out.at[t], sems.at[t]))
        copies[-1].start()
    for copy in copies:
        copy.wait()


def on_device(sizes, tracers, offsets, fraction, courant_north):
    tracer_count, level_count, rows, lanes = tracers.shape
    depth = tracer_count * level_count
    f32 = jnp.float32
    groups = rows // SUB
    slots = lanes // RIM
    tiles = -(-(depth * groups) // slots)
    column_tiles = -(-groups // slots)
    anywhere = pl.BlockSpec(memory_space=pl.ANY)
    vmem = pl.BlockSpec(memory_space=pltpu.VMEM)
    packed = pltpu.VMEM((tiles, SUB, lanes), f32)
    columns = pltpu.VMEM((column_tiles, SUB, lanes), f32)
    block = pltpu.VMEM((depth, rows, lanes), f32)
    two_blocks = pltpu.VMEM((2, depth, rows, lanes), f32)
    after, courant = pl.pallas_call(
        functools.partial(zonal_kernel, sizes),
        out_shape=(
            pltpu.VMEM((depth, rows + 2 * SUB, lanes), f32),
            pltpu.VMEM((rows + SUB, lanes), f32),
        ),
        in_specs=[pl.BlockSpec(memory_space=pltpu.HBM)] * 4,
        out_specs=(vmem, vmem),
        scratch_shapes=[
            two_blocks,
            pltpu.VMEM((rows, lanes), jnp.int32),
            pltpu.VMEM((rows, lanes), f32),
            block,
            packed, columns, packed, columns, packed,
            block, two_blocks, two_blocks, block,
            packed, packed, packed, packed, packed, packed,
            pltpu.SemaphoreType.DMA((4,)),
            pltpu.SemaphoreType.DMA((8,)),
            pltpu.SemaphoreType.DMA((8,)),
        ],
        compiler_params=pltpu.CompilerParams(collective_id=0, has_side_effects=True, vmem_limit_bytes=66_633_728),
    )(tracers.reshape(depth, rows, lanes), offsets, fraction, courant_north)
    advected = pl.pallas_call(
        merid_kernel,
        out_shape=jax.ShapeDtypeStruct((depth, rows, lanes), f32),
        in_specs=[vmem, vmem],
        out_specs=anywhere,
        scratch_shapes=[
            pltpu.VMEM((depth, rows + SUB, lanes), f32),
            pltpu.VMEM((depth, rows + SUB, lanes), f32),
            block,
            pltpu.SemaphoreType.DMA((depth,)),
        ],
        compiler_params=pltpu.CompilerParams(vmem_limit_bytes=8 << 20),
    )(after, courant)
    return advected.reshape(tracers.shape)


def solution(mesh):
    placed = (P(None, None, "lat", "lon"), P("lat", "lon"), P("lat", "lon"), P("lat", "lon"))
    return jax.shard_map(
        functools.partial(on_device, (mesh.shape["lat"], mesh.shape["lon"])),
        mesh=mesh,
        in_specs=placed,
        out_specs=P(None, None, "lat", "lon"),
        check_vma=False,
    )
```

time: 26.1 us -> 21.9 us (0.84)
  the two profiles are of different devices: /device:TPU:64 before, /device:TPU:32 now
where the time goes in v2:
time: 21.9 us; the launch traced here: 21.8 us
  Pallas kernels  21.8 us (100%)
    pallas_call x1, Pallas kernels, on_device(): pl.pallas_call(functools.partial(zonal_kernel, sizes), out_shape=(pltpu.V...  20.9 us
    pallas_call x1, Pallas kernels, on_device(): pl.pallas_call(merid_kernel, out_shape=jax.ShapeDtypeStruct((depth, rows,...  0.92 us

profile of v2, /device:TPU:32, one launch (start us, length us, event | category | flops | bytes accessed | tf_op | source)
XLA Modules:
  0.0 21.8 jit_solution(370409675529558942)
XLA Ops:
  0.0 20.9 %shard_map.46 = (f32[5,112,128]{2,1,0:T(8,128)S(1)}, f32[104,128]{1,0:T(8,128)S(1)}) custom-call(f32[5,96,128]{2,1,0:T(8,128)} %bitcast.4, s32[96,128]{1,0:T(8,128)} %off_in.1, f32[96,128]{1,0:T(8,128)} %fr_in.1, f32[96,128]{1,0:T(8,128)} %cn_in.1), custom_call_target="tpu_custom_call" | custom-call | tf_op jit(solution)/shard_map/pallas_call | solution.py:397
  20.9 0.9 %shard_map.47 = f32[5,96,128]{2,1,0:T(8,128)} custom-call(f32[5,112,128]{2,1,0:T(8,128)S(1)} %get-tuple-element.7.after, f32[104,128]{1,0:T(8,128)S(1)} %get-tuple-element.8.cn_buf), custom_call_target="tpu_custom_call" | custom-call | tf_op jit(solution)/shard_map/pallas_call | solution.py:419

commit v3 on v2

--- a/solution.py
+++ b/solution.py
@@ -63,7 +63,7 @@
 def zonal_kernel(
     sizes, tr, off_in, fr_in, cn_in, after, cn_buf,
     buf, off_buf, fr_buf, west_two, pack, ecol, got_pack, got_ecol, got_far,
-    lo_buf, prefix, total, suffix, own_head, halo, east_flux_buf, low_left, low_right, low_sum,
+    lo_buf, prefix, total, suffix, own_head, halo, east_flux_buf, low_left, low_right, low_sum, low_cell,
     local_sem, send_sem, recv_sem,
 ):
     lat_count, lon_count = sizes
@@ -200,27 +200,28 @@
         own_head[tile] = heads(ecol, tile)
     local[3].wait()
 
-    for copy in rim_copies:
-        copy.wait()
-
-    got_sum = split_dot(got_pack[...].reshape(tiles * SUB, lanes), slot_matrix)
-    for tile in range(tiles):
-        base, t = slot_pattern(tile, 0)
-        columns = got_ecol[tile * slots // (depth * slots)]
-        ahead = heads(got_ecol, tile)
-        tail = pack[tile]
-        left, right = packed_edges(tail, ahead, in_slot)
-        depart = take(columns, base + 2 * depth).astype(jnp.int32)
-        courant = take(columns, base + 2 * depth + 1)
-        index = (slot_of * RIM + (RIM - 1) - depart) & (lanes - 1)
-        span = slice(tile * SUB, (tile + 1) * SUB)
-        east_flux_buf[tile] = frac_flux(courant, take(right, index), take(left, index), take(tail, index)) - take(
-            tail_sum[span], index
-        )
-        west = got_pack[tile]
-        low_left[tile], low_right[tile] = packed_edges(west, own_head[tile], in_slot)
-        low_sum[tile] = got_sum[span]
-        halo[tile] = jnp.where(in_slot < 2, ahead, west)
+    def arrive():
+        for copy in rim_copies:
+            copy.wait()
+        got_sum = split_dot(got_pack[...].reshape(tiles * SUB, lanes), slot_matrix)
+        for tile in range(tiles):
+            base, t = slot_pattern(tile, 0)
+            columns = got_ecol[tile * slots // (depth * slots)]
+            ahead = heads(got_ecol, tile)
+            tail = pack[tile]
+            left, right = packed_edges(tail, ahead, in_slot)
+            depart = take(columns, base + 2 * depth).astype(jnp.int32)
+            courant = take(columns, base + 2 * depth + 1)
+            index = (slot_of * RIM + (RIM - 1) - depart) & (lanes - 1)
+            span = slice(tile * SUB, (tile + 1) * SUB)
+            east_flux_buf[tile] = frac_flux(courant, take(right, index), take(left, index), take(tail, index)) - take(
+                tail_sum[span], index
+            )
+            west = got_pack[tile]
+            low_left[tile], low_right[tile] = packed_edges(west, own_head[tile], in_slot)
+            low_sum[tile] = got_sum[span]
+            halo[tile] = jnp.where(in_slot < 2, ahead, west)
+            low_cell[tile] = west
 
     def finish(t, first, own, flux, east_flux):
         next_flux = roll(jnp.where(lane == 0, east_flux, flux), -1)
@@ -248,7 +249,7 @@
             flux = (
                 (own_prefix - own)
                 - pick(own_prefix, low_sum)
-                + frac_flux(courant, pick(right, low_right), pick(left, low_left), pick(own, got_pack))
+                + frac_flux(courant, pick(right, low_right), pick(left, low_left), pick(own, low_cell))
             )
             east_flux = take(east_flux_buf[tile], jnp.full((SUB, lanes), 0, jnp.int32) + slot * RIM)
             finish(t, first, own, flux, east_flux)
@@ -300,22 +301,26 @@
             )
             finish(t, first, own, flux, east_flux)
 
-    near_zonal(jnp.where(south_end, groups - 1, 0))
-    near_zonal(jnp.where(north_end, 1, jnp.where(south_end, groups - 2, groups - 1)))
+    edge_one = jnp.where(south_end, groups - 1, 0)
+    edge_two = jnp.where(north_end, 1, jnp.where(south_end, groups - 2, groups - 1))
     to_south = remote(after.at[:, pl.ds(SUB, SUB)], after.at[:, pl.ds(SUB + rows, SUB)], 6, lat_dev(-1))
     to_north = remote(after.at[:, pl.ds(rows, SUB)], after.at[:, pl.ds(0, SUB)], 7, lat_dev(1))
-    pl.when(has_south)(to_south.start)
-    pl.when(has_north)(to_north.start)
-
     inner = jnp.where(south_end, FULL_GROUPS, jnp.where(north_end, 2, 1))
     pairs = jnp.where(polar, (groups - FULL_GROUPS) // 2 - 1, groups // 2 - 1)
 
-    def inner_pair(i, carry):
-        near_zonal(inner + 2 * i)
-        near_zonal(inner + 2 * i + 1)
+    def pair(i, carry):
+        pl.when(i == 1)(arrive)
+        near_zonal(jnp.where(i < 2, edge_one, inner + 2 * i - 4))
+        near_zonal(jnp.where(i < 2, edge_two, inner + 2 * i - 3))
+
+        @pl.when(i == 1)
+        def _():
+            pl.when(has_south)(to_south.start)
+            pl.when(has_north)(to_north.start)
+
         return carry
 
-    lax.fori_loop(0, pairs, inner_pair, 0)
+    lax.fori_loop(0, pairs + 2, pair, 0)
 
     @pl.when(polar)
     def _():
@@ -409,7 +414,7 @@
             block,
             packed, columns, packed, columns, packed,
             block, two_blocks, two_blocks, block,
-            packed, packed, packed, packed, packed, packed,
+            packed, packed, packed, packed, packed, packed, packed,
             pltpu.SemaphoreType.DMA((4,)),
             pltpu.SemaphoreType.DMA((8,)),
             pltpu.SemaphoreType.DMA((8,)),

time: 21.9 us -> 21.1 us (0.963)
  Pallas kernels: 21.8 us -> 21 us
    pallas_call x1, Pallas kernels: 20.9 us -> 20.1 us  [on_device(): pl.pallas_call(functools.partial(zonal_kernel, sizes), out_shape=(pltpu.V...]
where the time goes in v3:
time: 21.1 us; the launch traced here: 21 us
  Pallas kernels  21 us (100%)
    pallas_call x1, Pallas kernels, on_device(): pl.pallas_call(functools.partial(zonal_kernel, sizes), out_shape=(pltpu.V...  20.1 us
    pallas_call x1, Pallas kernels, on_device(): pl.pallas_call(merid_kernel, out_shape=jax.ShapeDtypeStruct((depth, rows,...  0.92 us

profile of v3, /device:TPU:32, one launch (start us, length us, event | category | flops | bytes accessed | tf_op | source)
XLA Modules:
  0.0 21.0 jit_solution(9524210598177613842)
XLA Ops:
  0.0 20.1 %shard_map.46 = (f32[5,112,128]{2,1,0:T(8,128)S(1)}, f32[104,128]{1,0:T(8,128)S(1)}) custom-call(f32[5,96,128]{2,1,0:T(8,128)} %bitcast.4, s32[96,128]{1,0:T(8,128)} %off_in.1, f32[96,128]{1,0:T(8,128)} %fr_in.1, f32[96,128]{1,0:T(8,128)} %cn_in.1), custom_call_target="tpu_custom_call" | custom-call | tf_op jit(solution)/shard_map/pallas_call | solution.py:402
  20.1 0.9 %shard_map.47 = f32[5,96,128]{2,1,0:T(8,128)} custom-call(f32[5,112,128]{2,1,0:T(8,128)S(1)} %get-tuple-element.7.after, f32[104,128]{1,0:T(8,128)S(1)} %get-tuple-element.8.cn_buf), custom_call_target="tpu_custom_call" | custom-call | tf_op jit(solution)/shard_map/pallas_call | solution.py:424

commit v4 on v3

--- a/solution.py
+++ b/solution.py
@@ -153,12 +153,18 @@
     polar_row = jnp.where(south_end, 0, rows - POLAR_GROUPS * SUB)
     polar_span = pl.ds(pl.multiple_of(polar_row, SUB), POLAR_GROUPS * SUB)
     far_span = pl.ds(jnp.where(south_end, 0, tiles - 3), 3)
-    rim_copies = [
-        remote(pack, got_pack, 0, lon_dev(1)),
-        remote(ecol, got_ecol, 1, lon_dev(-1)),
-    ]
+    edge_parts = ((0, 2), (tiles - 2, tiles))
+    inner_part = (2, tiles - 2)
+
+    def rim_copy(part, index):
+        span = pl.ds(part[0], part[1] - part[0])
+        return remote(pack.at[span], got_pack.at[span], index, lon_dev(1))
+
+    rim_copies = [rim_copy(edge_parts[0], 0), rim_copy(edge_parts[1], 8), remote(ecol, got_ecol, 1, lon_dev(-1))]
+    inner_copy = rim_copy(inner_part, 9)
     for copy in rim_copies:
         copy.start()
+    inner_copy.start()
     polar_copies = [
         remote(tr.at[:, full_span], buf.at[1, :, full_span], 3, lon_dev(1)),
         remote(tr.at[:, polar_span], west_two.at[:, polar_span], 4, lon_dev(2)),
@@ -200,11 +206,10 @@
         own_head[tile] = heads(ecol, tile)
     local[3].wait()
 
-    def arrive():
-        for copy in rim_copies:
-            copy.wait()
-        got_sum = split_dot(got_pack[...].reshape(tiles * SUB, lanes), slot_matrix)
-        for tile in range(tiles):
+    def rim_tables(part):
+        first_tile, last_tile = part
+        got_sum = split_dot(got_pack[first_tile:last_tile].reshape((last_tile - first_tile) * SUB, lanes), slot_matrix)
+        for tile in range(first_tile, last_tile):
             base, t = slot_pattern(tile, 0)
             columns = got_ecol[tile * slots // (depth * slots)]
             ahead = heads(got_ecol, tile)
@@ -213,15 +218,24 @@
             depart = take(columns, base + 2 * depth).astype(jnp.int32)
             courant = take(columns, base + 2 * depth + 1)
             index = (slot_of * RIM + (RIM - 1) - depart) & (lanes - 1)
-            span = slice(tile * SUB, (tile + 1) * SUB)
-            east_flux_buf[tile] = frac_flux(courant, take(right, index), take(left, index), take(tail, index)) - take(
-                tail_sum[span], index
-            )
+            east_flux_buf[tile] = frac_flux(
+                courant, take(right, index), take(left, index), take(tail, index)
+            ) - take(tail_sum[tile * SUB : (tile + 1) * SUB], index)
             west = got_pack[tile]
             low_left[tile], low_right[tile] = packed_edges(west, own_head[tile], in_slot)
-            low_sum[tile] = got_sum[span]
+            low_sum[tile] = got_sum[(tile - first_tile) * SUB : (tile - first_tile + 1) * SUB]
             halo[tile] = jnp.where(in_slot < 2, ahead, west)
             low_cell[tile] = west
+
+    def arrive():
+        for copy in rim_copies:
+            copy.wait()
+        for part in edge_parts:
+            rim_tables(part)
+
+    def arrive_rest():
+        inner_copy.wait()
+        rim_tables(inner_part)
 
     def finish(t, first, own, flux, east_flux):
         next_flux = roll(jnp.where(lane == 0, east_flux, flux), -1)
@@ -310,6 +324,7 @@
 
     def pair(i, carry):
         pl.when(i == 1)(arrive)
+        pl.when(i == 2)(arrive_rest)
         near_zonal(jnp.where(i < 2, edge_one, inner + 2 * i - 4))
         near_zonal(jnp.where(i < 2, edge_two, inner + 2 * i - 3))
 
@@ -416,8 +431,8 @@
             block, two_blocks, two_blocks, block,
             packed, packed, packed, packed, packed, packed, packed,
             pltpu.SemaphoreType.DMA((4,)),
-            pltpu.SemaphoreType.DMA((8,)),
-            pltpu.SemaphoreType.DMA((8,)),
+            pltpu.SemaphoreType.DMA((10,)),
+            pltpu.SemaphoreType.DMA((10,)),
         ],
         compiler_params=pltpu.CompilerParams(collective_id=0, has_side_effects=True, vmem_limit_bytes=66_633_728),
     )(tracers.reshape(depth, rows, lanes), offsets, fraction, courant_north)

time: 21.1 us -> 20.9 us (level)
  no operation moved by 1% of the time
where the time goes in v4:
time: 20.9 us; the launch traced here: 20.8 us
  Pallas kernels  20.8 us (100%)
    pallas_call x1, Pallas kernels, on_device(): pl.pallas_call(functools.partial(zonal_kernel, sizes), out_shape=(pltpu.V...  19.9 us
    pallas_call x1, Pallas kernels, on_device(): pl.pallas_call(merid_kernel, out_shape=jax.ShapeDtypeStruct((depth, rows,...  0.92 us

profile of v4, /device:TPU:32, one launch (start us, length us, event | category | flops | bytes accessed | tf_op | source)
XLA Modules:
  0.0 20.8 jit_solution(11779625857769975202)
XLA Ops:
  0.0 19.9 %shard_map.46 = (f32[5,112,128]{2,1,0:T(8,128)S(1)}, f32[104,128]{1,0:T(8,128)S(1)}) custom-call(f32[5,96,128]{2,1,0:T(8,128)} %bitcast.4, s32[96,128]{1,0:T(8,128)} %off_in.1, f32[96,128]{1,0:T(8,128)} %fr_in.1, f32[96,128]{1,0:T(8,128)} %cn_in.1), custom_call_target="tpu_custom_call" | custom-call | tf_op jit(solution)/shard_map/pallas_call | solution.py:417
  19.9 0.9 %shard_map.47 = f32[5,96,128]{2,1,0:T(8,128)} custom-call(f32[5,112,128]{2,1,0:T(8,128)S(1)} %get-tuple-element.7.after, f32[104,128]{1,0:T(8,128)S(1)} %get-tuple-element.8.cn_buf), custom_call_target="tpu_custom_call" | custom-call | tf_op jit(solution)/shard_map/pallas_call | solution.py:439

commit v5 on v4

--- a/solution.py
+++ b/solution.py
@@ -60,9 +60,9 @@
     return left, right
 
 
-def zonal_kernel(
-    sizes, tr, off_in, fr_in, cn_in, after, cn_buf,
-    buf, off_buf, fr_buf, west_two, pack, ecol, got_pack, got_ecol, got_far,
+def step_kernel(
+    sizes, tr, off_in, fr_in, cn_in, done,
+    after, cn_buf, edge_buf, flux_buf, buf, off_buf, fr_buf, west_two, pack, ecol, got_pack, got_ecol, got_far,
     lo_buf, prefix, total, suffix, own_head, halo, east_flux_buf, low_left, low_right, low_sum, low_cell,
     local_sem, send_sem, recv_sem,
 ):
@@ -356,6 +356,27 @@
 
         lax.fori_loop(0, FULL_GROUPS // 2, full_pair, 0)
 
+    def merid(t, first, count):
+        at = first + SUB
+        edge_buf[t, at - 1 : at + count + 1, :] = wide_weight * (
+            after[t, at - 2 : at + count, :] + after[t, at - 1 : at + count + 1, :]
+        ) - narrow_weight * (after[t, at - 3 : at + count - 1, :] + after[t, at : at + count + 2, :])
+        flux_buf[t, first : first + count + 1, :] = frac_flux(
+            cn_buf[first : first + count + 1, :],
+            edge_buf[t, at : at + count + 1, :],
+            edge_buf[t, at - 1 : at + count, :],
+            after[t, at - 1 : at + count, :],
+        )
+        done[t, first : first + count, :] = after[t, at : at + count, :] - (
+            flux_buf[t, first + 1 : first + count + 1, :] - flux_buf[t, first : first + count, :]
+        )
+
+    def merid_inner(t, carry):
+        merid(t, SUB, rows - 2 * SUB)
+        return carry
+
+    lax.fori_loop(0, depth, merid_inner, 0)
+
     @pl.when(has_south)
     def _():
         courant_copy.wait_send()
@@ -378,26 +399,18 @@
         after[:, SUB + rows :, :] = jnp.zeros((depth, SUB, lanes), jnp.float32)
         cn_buf[rows:, :] = jnp.zeros((SUB, lanes), jnp.float32)
 
-
-def merid_kernel(after, cn_buf, out, edge_buf, flux_buf, done, sems):
-    depth, rows, lanes = out.shape
-    courant = cn_buf[0 : rows + 1, :]
-    copies = []
-    for t in range(depth):
-        edge_buf[t, 0 : rows + 2, :] = wide_weight * (
-            after[t, SUB - 2 : SUB + rows, :] + after[t, SUB - 1 : SUB + rows + 1, :]
-        ) - narrow_weight * (after[t, SUB - 3 : SUB + rows - 1, :] + after[t, SUB : SUB + rows + 2, :])
-        flux_buf[t, 0 : rows + 1, :] = frac_flux(
-            courant,
-            edge_buf[t, 1 : rows + 2, :],
-            edge_buf[t, 0 : rows + 1, :],
-            after[t, SUB - 1 : SUB + rows, :],
-        )
-        done[t] = after[t, SUB : SUB + rows, :] - (flux_buf[t, 1 : rows + 1, :] - flux_buf[t, 0:rows, :])
-        copies.append(pltpu.make_async_copy(done.at[t], out.at[t], sems.at[t]))
-        copies[-1].start()
-    for copy in copies:
-        copy.wait()
+    def merid_rim(t, carry):
+        merid(t, 0, SUB)
+        merid(t, rows - SUB, SUB)
+        return carry
+
+    lax.fori_loop(0, depth, merid_rim, 0)
+
+
+def store_kernel(done, out, sem):
+    copy = pltpu.make_async_copy(done, out, sem)
+    copy.start()
+    copy.wait()
 
 
 def on_device(sizes, tracers, offsets, fraction, courant_north):
@@ -414,15 +427,16 @@
     columns = pltpu.VMEM((column_tiles, SUB, lanes), f32)
     block = pltpu.VMEM((depth, rows, lanes), f32)
     two_blocks = pltpu.VMEM((2, depth, rows, lanes), f32)
-    after, courant = pl.pallas_call(
-        functools.partial(zonal_kernel, sizes),
-        out_shape=(
+    done = pl.pallas_call(
+        functools.partial(step_kernel, sizes),
+        out_shape=pltpu.VMEM((depth, rows, lanes), f32),
+        in_specs=[pl.BlockSpec(memory_space=pltpu.HBM)] * 4,
+        out_specs=vmem,
+        scratch_shapes=[
             pltpu.VMEM((depth, rows + 2 * SUB, lanes), f32),
             pltpu.VMEM((rows + SUB, lanes), f32),
-        ),
-        in_specs=[pl.BlockSpec(memory_space=pltpu.HBM)] * 4,
-        out_specs=(vmem, vmem),
-        scratch_shapes=[
+            pltpu.VMEM((depth, rows + 2 * SUB, lanes), f32),
+            pltpu.VMEM((depth, rows + SUB, lanes), f32),
             two_blocks,
             pltpu.VMEM((rows, lanes), jnp.int32),
             pltpu.VMEM((rows, lanes), f32),
@@ -434,21 +448,16 @@
             pltpu.SemaphoreType.DMA((10,)),
             pltpu.SemaphoreType.DMA((10,)),
         ],
-        compiler_params=pltpu.CompilerParams(collective_id=0, has_side_effects=True, vmem_limit_bytes=66_633_728),
+        compiler_params=pltpu.CompilerParams(collective_id=0, has_side_effects=True, vmem_limit_bytes=66_747_392),
     )(tracers.reshape(depth, rows, lanes), offsets, fraction, courant_north)
     advected = pl.pallas_call(
-        merid_kernel,
+        store_kernel,
         out_shape=jax.ShapeDtypeStruct((depth, rows, lanes), f32),
-        in_specs=[vmem, vmem],
+        in_specs=[vmem],
         out_specs=anywhere,
-        scratch_shapes=[
-            pltpu.VMEM((depth, rows + SUB, lanes), f32),
-            pltpu.VMEM((depth, rows + SUB, lanes), f32),
-            block,
-            pltpu.SemaphoreType.DMA((depth,)),
-        ],
+        scratch_shapes=[pltpu.SemaphoreType.DMA],
         compiler_params=pltpu.CompilerParams(vmem_limit_bytes=8 << 20),
-    )(after, courant)
+    )(done)
     return advected.reshape(tracers.shape)
 
 

time: 20.9 us -> 20.9 us (level)
  no operation moved by 1% of the time
where the time goes in v5:
time: 20.9 us; the launch traced here: 20.8 us
  Pallas kernels  20.7 us (99%)
    pallas_call x1, Pallas kernels, on_device(): pl.pallas_call(functools.partial(step_kernel, sizes), out_shape=pltpu.VME...  20 us
    pallas_call x1, Pallas kernels, on_device(): pl.pallas_call(store_kernel, out_shape=jax.ShapeDtypeStruct((depth, rows,...  0.7 us

profile of v5, /device:TPU:32, one launch (start us, length us, event | category | flops | bytes accessed | tf_op | source)
XLA Modules:
  0.0 20.8 jit_solution(7057857879516415504)
XLA Ops:
  0.0 20.0 %shard_map.46.done = f32[5,96,128]{2,1,0:T(8,128)S(1)} custom-call(f32[5,96,128]{2,1,0:T(8,128)} %bitcast.4, s32[96,128]{1,0:T(8,128)} %off_in.1, f32[96,128]{1,0:T(8,128)} %fr_in.1, f32[96,128]{1,0:T(8,128)} %cn_in.1), custom_call_target="tpu_custom_call" | custom-call | tf_op jit(solution)/shard_map/pallas_call | solution.py:430
  20.1 0.7 %shard_map.47 = f32[5,96,128]{2,1,0:T(8,128)} custom-call(f32[5,96,128]{2,1,0:T(8,128)S(1)} %shard_map.46.done), custom_call_target="tpu_custom_call" | custom-call | tf_op jit(solution)/shard_map/pallas_call | solution.py:453

commit v6 on v5

--- a/solution.py
+++ b/solution.py
@@ -317,8 +317,8 @@
 
     edge_one = jnp.where(south_end, groups - 1, 0)
     edge_two = jnp.where(north_end, 1, jnp.where(south_end, groups - 2, groups - 1))
-    to_south = remote(after.at[:, pl.ds(SUB, SUB)], after.at[:, pl.ds(SUB + rows, SUB)], 6, lat_dev(-1))
-    to_north = remote(after.at[:, pl.ds(rows, SUB)], after.at[:, pl.ds(0, SUB)], 7, lat_dev(1))
+    to_south = remote(after.at[:, pl.ds(SUB, 2)], after.at[:, pl.ds(SUB + rows, 2)], 6, lat_dev(-1))
+    to_north = remote(after.at[:, pl.ds(SUB + rows - 3, 3)], after.at[:, pl.ds(SUB - 3, 3)], 7, lat_dev(1))
     inner = jnp.where(south_end, FULL_GROUPS, jnp.where(north_end, 2, 1))
     pairs = jnp.where(polar, (groups - FULL_GROUPS) // 2 - 1, groups // 2 - 1)
 

time: 20.9 us -> 20.7 us (level)
  no operation moved by 1% of the time
where the time goes in v6:
time: 20.7 us; the launch traced here: 20.6 us
  Pallas kernels  20.6 us (100%)
    pallas_call x1, Pallas kernels, on_device(): pl.pallas_call(functools.partial(step_kernel, sizes), out_shape=pltpu.VME...  19.9 us
    pallas_call x1, Pallas kernels, on_device(): pl.pallas_call(store_kernel, out_shape=jax.ShapeDtypeStruct((depth, rows,...  0.7 us

profile of v6, /device:TPU:32, one launch (start us, length us, event | category | flops | bytes accessed | tf_op | source)
XLA Modules:
  0.0 20.6 jit_solution(15853547703820225597)
XLA Ops:
  0.0 19.9 %shard_map.46.done = f32[5,96,128]{2,1,0:T(8,128)S(1)} custom-call(f32[5,96,128]{2,1,0:T(8,128)} %bitcast.4, s32[96,128]{1,0:T(8,128)} %off_in.1, f32[96,128]{1,0:T(8,128)} %fr_in.1, f32[96,128]{1,0:T(8,128)} %cn_in.1), custom_call_target="tpu_custom_call" | custom-call | tf_op jit(solution)/shard_map/pallas_call | solution.py:430
  19.9 0.7 %shard_map.47 = f32[5,96,128]{2,1,0:T(8,128)} custom-call(f32[5,96,128]{2,1,0:T(8,128)S(1)} %shard_map.46.done), custom_call_target="tpu_custom_call" | custom-call | tf_op jit(solution)/shard_map/pallas_call | solution.py:453

commit v7 on v5

--- a/solution.py
+++ b/solution.py
@@ -115,15 +115,22 @@
     for copy in local[:3]:
         copy.wait()
 
-    for tile in range(tiles):
-        packed = jnp.zeros((SUB, lanes), jnp.float32)
-        for slot in range(slots):
-            group, t = divmod(tile * slots + slot, depth)
-            if group >= groups:
-                break
-            cells = buf[0, t, group * SUB : (group + 1) * SUB, :]
-            packed = jnp.where(slot_of == slot, roll(cells, RIM * (slot + 1)), packed)
-        pack[tile] = packed
+    edge_parts = ((0, 2), (tiles - 2, tiles))
+    inner_part = (2, tiles - 2)
+
+    def pack_rims(part):
+        for tile in range(*part):
+            packed = jnp.zeros((SUB, lanes), jnp.float32)
+            for slot in range(slots):
+                group, t = divmod(tile * slots + slot, depth)
+                if group >= groups:
+                    break
+                cells = buf[0, t, group * SUB : (group + 1) * SUB, :]
+                packed = jnp.where(slot_of == slot, roll(cells, RIM * (slot + 1)), packed)
+            pack[tile] = packed
+
+    for part in edge_parts:
+        pack_rims(part)
     for tile in range(ecol.shape[0]):
         packed = jnp.zeros((SUB, lanes), jnp.float32)
         for slot in range(slots):
@@ -153,9 +160,6 @@
     polar_row = jnp.where(south_end, 0, rows - POLAR_GROUPS * SUB)
     polar_span = pl.ds(pl.multiple_of(polar_row, SUB), POLAR_GROUPS * SUB)
     far_span = pl.ds(jnp.where(south_end, 0, tiles - 3), 3)
-    edge_parts = ((0, 2), (tiles - 2, tiles))
-    inner_part = (2, tiles - 2)
-
     def rim_copy(part, index):
         span = pl.ds(part[0], part[1] - part[0])
         return remote(pack.at[span], got_pack.at[span], index, lon_dev(1))
@@ -164,6 +168,7 @@
     inner_copy = rim_copy(inner_part, 9)
     for copy in rim_copies:
         copy.start()
+    pack_rims(inner_part)
     inner_copy.start()
     polar_copies = [
         remote(tr.at[:, full_span], buf.at[1, :, full_span], 3, lon_dev(1)),

time: 20.9 us -> 20.9 us (level)
  no operation moved by 1% of the time
where the time goes in v7:
time: 20.9 us; the launch traced here: 20.8 us
  Pallas kernels  20.8 us (100%)
    pallas_call x1, Pallas kernels, on_device(): pl.pallas_call(functools.partial(step_kernel, sizes), out_shape=pltpu.VME...  20 us
    pallas_call x1, Pallas kernels, on_device(): pl.pallas_call(store_kernel, out_shape=jax.ShapeDtypeStruct((depth, rows,...  0.7 us

profile of v7, /device:TPU:32, one launch (start us, length us, event | category | flops | bytes accessed | tf_op | source)
XLA Modules:
  0.0 20.8 jit_solution(13927746770157350843)
XLA Ops:
  0.0 20.0 %shard_map.46.done = f32[5,96,128]{2,1,0:T(8,128)S(1)} custom-call(f32[5,96,128]{2,1,0:T(8,128)} %bitcast.4, s32[96,128]{1,0:T(8,128)} %off_in.1, f32[96,128]{1,0:T(8,128)} %fr_in.1, f32[96,128]{1,0:T(8,128)} %cn_in.1), custom_call_target="tpu_custom_call" | custom-call | tf_op jit(solution)/shard_map/pallas_call | solution.py:435
  20.1 0.7 %shard_map.47 = f32[5,96,128]{2,1,0:T(8,128)} custom-call(f32[5,96,128]{2,1,0:T(8,128)S(1)} %shard_map.46.done), custom_call_target="tpu_custom_call" | custom-call | tf_op jit(solution)/shard_map/pallas_call | solution.py:458

commit v8 on v5

--- a/solution.py
+++ b/solution.py
@@ -408,9 +408,11 @@
 
 
 def store_kernel(done, out, sem):
-    copy = pltpu.make_async_copy(done, out, sem)
-    copy.start()
-    copy.wait()
+    copies = [pltpu.make_async_copy(done.at[t], out.at[t], sem.at[t]) for t in range(out.shape[0])]
+    for copy in copies:
+        copy.start()
+    for copy in copies:
+        copy.wait()
 
 
 def on_device(sizes, tracers, offsets, fraction, courant_north):
@@ -455,7 +457,7 @@
         out_shape=jax.ShapeDtypeStruct((depth, rows, lanes), f32),
         in_specs=[vmem],
         out_specs=anywhere,
-        scratch_shapes=[pltpu.SemaphoreType.DMA],
+        scratch_shapes=[pltpu.SemaphoreType.DMA((depth,))],
         compiler_params=pltpu.CompilerParams(vmem_limit_bytes=8 << 20),
     )(done)
     return advected.reshape(tracers.shape)

time: 20.9 us -> 20.9 us (level)
  no operation moved by 1% of the time
where the time goes in v8:
time: 20.9 us; the launch traced here: 20.8 us
  Pallas kernels  20.8 us (100%)
    pallas_call x1, Pallas kernels, on_device(): pl.pallas_call(functools.partial(step_kernel, sizes), out_shape=pltpu.VME...  20 us
    pallas_call x1, Pallas kernels, on_device(): pl.pallas_call(store_kernel, out_shape=jax.ShapeDtypeStruct((depth, rows,...  0.73 us

profile of v8, /device:TPU:32, one launch (start us, length us, event | category | flops | bytes accessed | tf_op | source)
XLA Modules:
  0.0 20.8 jit_solution(7034625460103950946)
XLA Ops:
  0.0 20.0 %shard_map.46.done = f32[5,96,128]{2,1,0:T(8,128)S(1)} custom-call(f32[5,96,128]{2,1,0:T(8,128)} %bitcast.4, s32[96,128]{1,0:T(8,128)} %off_in.1, f32[96,128]{1,0:T(8,128)} %fr_in.1, f32[96,128]{1,0:T(8,128)} %cn_in.1), custom_call_target="tpu_custom_call" | custom-call | tf_op jit(solution)/shard_map/pallas_call | solution.py:432
  20.1 0.7 %shard_map.47 = f32[5,96,128]{2,1,0:T(8,128)} custom-call(f32[5,96,128]{2,1,0:T(8,128)S(1)} %shard_map.46.done), custom_call_target="tpu_custom_call" | custom-call | tf_op jit(solution)/shard_map/pallas_call | solution.py:455
